TPU v7x, 256 devices: a whole 4x4x8 slice. The times are simulated.
256 devices in a mesh: seq: 64 (over y, z_hi, x, core), dp: 4 (over z_lo).
Axes of the slice: x: 4, y: 4, z: 8 (z_hi: 2, z_lo: 4; z = z_hi * 4 + z_lo), core: 2. Of those that a mesh axis runs over, the one named last changes fastest.
Arguments:
- query: bfloat16 [4, 8192, 2048], P('dp', 'seq'), may hold values from -6 to 6
- keys: bfloat16 [4, 8192, 512], P('dp', 'seq'), may hold values from -6 to 6
- values: bfloat16 [4, 8192, 512], P('dp', 'seq'), may hold values from -6 to 6
- out_grad: bfloat16 [4, 8192, 2048], P('dp', 'seq'), may hold values from -16 to 16
- normed_input: bfloat16 [4, 8192, 4096], P('dp', 'seq'), may hold values from -16 to 16
- q_start: int32 [8], P('dp'), may hold values from 2048 to 3071, as said below
- q_len: int32 [8], P('dp'), may hold values from 1 to 512, as said below
Outputs:
- q_grad: bfloat16 [4, 8192, 2048], P('dp', 'seq')
- k_grad: bfloat16 [4, 8192, 512], P('dp', 'seq')
- v_grad: bfloat16 [4, 8192, 512], P('dp', 'seq')
- kv_weight_grad: float32 [4096, 1024], P(('seq', 'dp'))
Inputs may be any that keep to these rules, and one draw needn't show every extreme that they name: `q_start`: the visual part of each sequence ends here. `q_len`: tokens after the question are padding.
All inputs are finite; a program needn't handle non-finite values.
Results may differ from a plain program's by a relative error of at most 0.013.
Values may be sent and summed in bfloat16 or wider, within the bound.
A program may use at most 128 MiB of HBM per device.

v0:
```python
import math
import jax
import jax.numpy as jnp
from jax import lax
from jax.sharding import PartitionSpec as P

HEADS = 16
KV_HEADS = 4
HEAD_DIM = 128


def local(query, keys, values, out_grad, normed_input, q_start, q_len):
    seq_count = lax.axis_size("seq")
    tokens_dev = query.shape[1]
    repeat_by = HEADS // KV_HEADS
    classes = max(1, seq_count // HEADS)
    heads_dev = HEADS * classes // seq_count
    head_groups = seq_count // classes
    class_tokens = tokens_dev // classes
    seq_len = tokens_dev * seq_count // 2
    group_tokens = tokens_dev * seq_count
    width_dev = heads_dev * HEAD_DIM
    my_class = lax.axis_index("seq") // head_groups
    score_scale = 1.0 / math.sqrt(HEAD_DIM)

    def to_units(array):
        return array.reshape(class_tokens, seq_count, width_dev)

    query_units = to_units(query[0])
    grad_units = to_units(out_grad[0])
    key_wide = jnp.repeat(
        keys[0].reshape(tokens_dev, KV_HEADS, HEAD_DIM), repeat_by, axis=1
    ).reshape(tokens_dev, HEADS * HEAD_DIM)
    value_wide = jnp.repeat(
        values[0].reshape(tokens_dev, KV_HEADS, HEAD_DIM), repeat_by, axis=1
    ).reshape(tokens_dev, HEADS * HEAD_DIM)
    wide_shape = (tokens_dev, classes, head_groups, width_dev)
    key_units = jnp.broadcast_to(
        key_wide.reshape(tokens_dev, 1, head_groups, width_dev), wide_shape
    ).reshape(tokens_dev, seq_count, width_dev)
    value_units = jnp.broadcast_to(
        value_wide.reshape(tokens_dev, 1, head_groups, width_dev), wide_shape
    ).reshape(tokens_dev, seq_count, width_dev)
    query_got, grad_got, key_got, value_got = (
        lax.all_to_all(query_units, "seq", split_axis=1, concat_axis=0, tiled=True),
        lax.all_to_all(grad_units, "seq", split_axis=1, concat_axis=0, tiled=True),
        lax.all_to_all(key_units, "seq", split_axis=1, concat_axis=0, tiled=True),
        lax.all_to_all(value_units, "seq", split_axis=1, concat_axis=0, tiled=True),
    )
    block_rows = min(512, seq_len // classes)
    blocks_seq = seq_len // classes // block_rows
    key_pos = jnp.arange(seq_len, dtype=jnp.int32)

    def one_block(block_idx, carry):
        query_acc, key_acc, value_acc = carry
        seq_idx = block_idx // blocks_seq
        first_row = block_idx * block_rows
        key_first = seq_idx * seq_len
        query_block = lax.dynamic_slice_in_dim(query_got, first_row, block_rows, 0)
        grad_block = lax.dynamic_slice_in_dim(grad_got, first_row, block_rows, 0)
        key_block = lax.dynamic_slice_in_dim(key_got, key_first, seq_len, 0)
        value_block = lax.dynamic_slice_in_dim(value_got, key_first, seq_len, 0)
        start_pos = lax.dynamic_index_in_dim(q_start, seq_idx, 0, keepdims=False)
        end_pos = start_pos + lax.dynamic_index_in_dim(q_len, seq_idx, 0, keepdims=False)
        query_pos = (
            (first_row + jnp.arange(block_rows, dtype=jnp.int32)) * classes + my_class - key_first
        )
        visible = (key_pos[None, :] < end_pos) & (
            (key_pos[None, :] <= query_pos[:, None]) | (key_pos[None, :] < start_pos)
        )
        scores = (
            jnp.einsum("qhd,khd->hqk", query_block, key_block, preferred_element_type=jnp.float32)
            * score_scale
        )
        scores = jnp.where(visible[None], scores, -jnp.inf)
        row_max = jnp.max(scores, axis=-1, keepdims=True)
        exponent = jnp.where(visible[None], jnp.exp(scores - row_max), 0.0)
        probability = exponent / jnp.sum(exponent, axis=-1, keepdims=True)
        prob_low = probability.astype(jnp.bfloat16)
        dprob = jnp.einsum(
            "qhd,khd->hqk", grad_block, value_block, preferred_element_type=jnp.float32
        )
        row_delta = jnp.sum(probability * dprob, axis=-1, keepdims=True)
        dscore = (probability * (dprob - row_delta) * score_scale).astype(jnp.bfloat16)
        query_grad = jnp.einsum(
            "hqk,khd->qhd", dscore, key_block, preferred_element_type=jnp.float32
        ).astype(jnp.bfloat16)
        query_acc = lax.dynamic_update_slice_in_dim(query_acc, query_grad, first_row, 0)
        key_part = lax.dynamic_slice_in_dim(key_acc, key_first, seq_len, 0) + jnp.einsum(
            "hqk,qhd->khd", dscore, query_block, preferred_element_type=jnp.float32
        )
        value_part = lax.dynamic_slice_in_dim(value_acc, key_first, seq_len, 0) + jnp.einsum(
            "hqk,qhd->khd", prob_low, grad_block, preferred_element_type=jnp.float32
        )
        key_acc = lax.dynamic_update_slice_in_dim(key_acc, key_part, key_first, 0)
        value_acc = lax.dynamic_update_slice_in_dim(value_acc, value_part, key_first, 0)
        return (query_acc, key_acc, value_acc)

    start_state = (
        jnp.zeros((seq_count * class_tokens, heads_dev, HEAD_DIM), jnp.bfloat16),
        jnp.zeros((group_tokens, heads_dev, HEAD_DIM), jnp.float32),
        jnp.zeros((group_tokens, heads_dev, HEAD_DIM), jnp.float32),
    )
    query_acc, key_acc, value_acc = lax.fori_loop(0, 2 * blocks_seq, one_block, start_state)
    query_back = lax.all_to_all(
        query_acc.reshape(seq_count, class_tokens, 1, width_dev),
        "seq",
        split_axis=0,
        concat_axis=2,
        tiled=True,
    )
    query_grad_out = query_back.reshape(tokens_dev, HEADS * HEAD_DIM)
    key_back, value_back = (
        lax.all_to_all(
            key_acc.reshape(seq_count, tokens_dev, 1, width_dev).astype(jnp.bfloat16),
            "seq",
            split_axis=0,
            concat_axis=2,
            tiled=True,
        ).astype(jnp.float32),
        lax.all_to_all(
            value_acc.reshape(seq_count, tokens_dev, 1, width_dev).astype(jnp.bfloat16),
            "seq",
            split_axis=0,
            concat_axis=2,
            tiled=True,
        ).astype(jnp.float32),
    )
    key_grad_out = (
        key_back.reshape(tokens_dev, classes, KV_HEADS, repeat_by, HEAD_DIM)
        .sum(axis=(1, 3))
        .astype(jnp.bfloat16)
        .reshape(tokens_dev, KV_HEADS * HEAD_DIM)
    )
    value_grad_out = (
        value_back.reshape(tokens_dev, classes, KV_HEADS, repeat_by, HEAD_DIM)
        .sum(axis=(1, 3))
        .astype(jnp.bfloat16)
        .reshape(tokens_dev, KV_HEADS * HEAD_DIM)
    )
    joined = jnp.concatenate([key_grad_out, value_grad_out], axis=1)
    hidden_rows = normed_input[0]
    weight_out = lax.psum_scatter(
        jnp.einsum("tr,tc->rc", hidden_rows, joined, preferred_element_type=jnp.float32),
        ("seq", "dp"),
        scatter_dimension=0,
        tiled=True,
    )
    return (query_grad_out[None], key_grad_out[None], value_grad_out[None], weight_out)


def solution(mesh):
    in_specs = (
        P("dp", "seq", None),
        P("dp", "seq", None),
        P("dp", "seq", None),
        P("dp", "seq", None),
        P("dp", "seq", None),
        P("dp"),
        P("dp"),
    )
    out_specs = (
        P("dp", "seq", None),
        P("dp", "seq", None),
        P("dp", "seq", None),
        P(("seq", "dp"), None),
    )
    return jax.shard_map(local, mesh=mesh, in_specs=in_specs, out_specs=out_specs, check_vma=False)
```

profile of v0, /device:TPU:0, one launch (start us, length us, event | category | flops | bytes accessed | tf_op | source)
XLA Modules:
  0.0 1879.8 jit_solution(11580417287337845989)
XLA Ops:
  9.7 12.8 all-to-all-start.2
  25.0 15.2 all-to-all-done.2
  40.2 4.6 all-to-all-start.1
  45.0 16.3 all-to-all-done.1
  63.3 8.7 all-to-all-start.3
  72.1 32.6 %all-to-all-done.3 = bf16[128,64,128]{2,0,1:T(8,128)(2,1)} async-done(((bf16[128,64,128]{2,0,1:T(8,128)(2,1)}), bf16[128,64,128]{2,0,1:T(8,128)(2,1)}, u32[]{:S(2)}, u32[]{:S(2)}) %all-to-all-start.3) | async-done | bytes 2097184 | tf_op jit(solution)/shard_map/all_to_all | solution.py:48
  106.7 25.7 %all-to-all-start = ((bf16[128,64,128]{2,0,1:T(8,128)(2,1)}), bf16[128,64,128]{2,0,1:T(8,128)(2,1)S(1)}, u32[]{:S(2)}, u32[]{:S(2)}) async-start(bf16[128,64,128]{2,0,1:T(8,128)(2,1)} %bitcast.133), calls=%async_computation | async-start | bytes 4194304 | tf_op jit(solution)/shard_map/all_to_all | solution.py:47
  132.4 32.8 %all-to-all-done = bf16[128,64,128]{2,0,1:T(8,128)(2,1)S(1)} async-done(((bf16[128,64,128]{2,0,1:T(8,128)(2,1)}), bf16[128,64,128]{2,0,1:T(8,128)(2,1)S(1)}, u32[]{:S(2)}, u32[]{:S(2)}) %all-to-all-start) | async-done | bytes 2097184 | tf_op jit(solution)/shard_map/all_to_all | solution.py:47
  170.6 244.7 %while.21 = (s32[]{:T(128)}, bf16[2048,1,128]{2,0,1:T(8,128)(2,1)}, f32[8192,1,128]{2,0,1:T(8,128)}, f32[8192,1,128]{2,0,1:T(8,128)}, bf16[8192,1,128]{2,0,1:T(8...) while((s32[]{:T(128)}, bf16[2048,1,128]{2,0,1:T(8,128)(2,1)}, ...), condition=%wide.region_4.5_spmd.clone.clone, body=%wide.region_0.4_spmd.clone.clone.sunk | while | flops 2746294784 | bytes 167959120 | solution.py:104
  173.8 3.8 fusion.57
  177.6 4.2 fusion.58
  181.9 9.4 multiply_reduce_fusion.2
  191.3 10.0 multiply_convert_fusion.2
  204.9 3.7 fusion.61
  210.4 3.1 constant_dynamic-slice_fusion.4
  215.4 5.5 fusion.60
  224.0 4.1 constant_dynamic-update-slice_fusion.6
  235.0 3.8 fusion.57
  238.8 4.2 fusion.58
  243.0 9.4 multiply_reduce_fusion.2
  252.5 10.0 multiply_convert_fusion.2
  266.1 3.7 fusion.61
  271.6 3.1 constant_dynamic-slice_fusion.4
  276.6 5.5 fusion.60
  285.2 4.1 constant_dynamic-update-slice_fusion.6
  296.1 3.8 fusion.57
  299.9 4.2 fusion.58
  304.2 9.4 multiply_reduce_fusion.2
  313.6 10.0 multiply_convert_fusion.2
  327.2 3.7 fusion.61
  337.7 5.5 fusion.60
  346.3 4.0 constant_dynamic-update-slice_fusion.6
  357.3 3.8 fusion.57
  361.1 4.2 fusion.58
  365.3 9.4 multiply_reduce_fusion.2
  374.8 10.0 multiply_convert_fusion.2
  388.4 3.7 fusion.61
  393.9 3.1 constant_dynamic-slice_fusion.4
  398.9 5.5 fusion.60
  407.5 4.0 constant_dynamic-update-slice_fusion.6
  420.5 20.8 %all-to-all-start.5 = ((bf16[64,128,1,128]{1,3,2,0:T(8,128)(2,1)}), bf16[64,128,1,128]{1,3,2,0:T(8,128)(2,1)}, u32[]{:S(2)}, u32[]{:S(2)}) async-start(bf16[64,128,1,128]{1,3,2,0:T(8,128)(2,1)} %copy.46), calls=%async_computation.5 | async-start | bytes 4194304 | tf_op jit(solution)/shard_map/all_to_all | solution.py:114
  446.6 27.3 %all-to-all-done.5 = bf16[64,128,1,128]{1,3,2,0:T(8,128)(2,1)} async-done(((bf16[64,128,1,128]{1,3,2,0:T(8,128)(2,1)}), bf16[64,128,1,128]{1,3,2,0:T(8,128)(2,1)}, u32[]{:S(2)}, u32[]{:S(2)}) %all-to-all-start.5) | async-done | bytes 2097184 | tf_op jit(solution)/shard_map/all_to_all | solution.py:114
  474.0 25.7 %all-to-all-start.6 = ((bf16[64,128,1,128]{1,3,2,0:T(8,128)(2,1)}), bf16[64,128,1,128]{1,3,2,0:T(8,128)(2,1)S(1)}, u32[]{:S(2)}, u32[]{:S(2)}) async-start(bf16[64,128,1,128]{1,3,2,0:T(8,128)(2,1)} %copy.50), calls=%async_computation.6 | async-start | bytes 4194304 | tf_op jit(solution)/shard_map/all_to_all | solution.py:121
  501.7 30.9 %all-to-all-done.6 = bf16[64,128,1,128]{1,3,2,0:T(8,128)(2,1)S(1)} async-done(((bf16[64,128,1,128]{1,3,2,0:T(8,128)(2,1)}), bf16[64,128,1,128]{1,3,2,0:T(8,128)(2,1)S(1)}, u32[]{:S(2)}, u32[]{:S(2)}) %all-to-all-start.6) | async-done | bytes 2097184 | tf_op jit(solution)/shard_map/all_to_all | solution.py:121
  532.9 8.1 convolution_bitcast_fusion.2
  541.0 17.4 copy.58
  559.4 36.8 %all_to_all.105 = bf16[64,32,1,128]{3,1,2,0:T(8,128)(2,1)S(1)} all-to-all(bf16[64,32,1,128]{3,1,2,0:T(8,128)(2,1)S(1)} %bitcast.139), channel_id=1, replica_groups=mesh['seq'=64,'dp'=4] {'seq'}, dimensions={0} | all-to-all | bytes 1048576 | tf_op jit(solution)/shard_map/all_to_all | solution.py:105
  599.0 1274.0 %reduce-scatter.4.cloned.1.call-done = f32[16,1024]{1,0:T(8,128)} async-done(((f32[4096,1024]{1,0:T(8,128)}), f32[16,1024]{1,0:T(8,128)}) %reduce-scatter.4.cloned.1.call-update) | async-done | bytes 65552
  (128 shorter events, 98.3 us)
Async XLA Ops:
  7.2 525.7 %copy-start = (bf16[1,128,4096]{2,1,0:T(8,128)(2,1)S(1)}, bf16[1,128,4096]{2,1,0:T(8,128)(2,1)}, u32[]{:S(2)}) copy-start(bf16[1,128,4096]{2,1,0:T(8,128)(2,1)} %param.13) | copy-start | bytes 3145732
  7.2 37.7 %copy-start.8 = (bf16[1,128,512]{2,1,0:T(8,128)(2,1)S(1)}, bf16[1,128,512]{2,1,0:T(8,128)(2,1)}, u32[]{:S(2)}) copy-start(bf16[1,128,512]{2,1,0:T(8,128)(2,1)} %param.11) | copy-start | bytes 393220
  9.7 30.5 %all-to-all-start.2 = ((bf16[32,64,128]{2,0,1:T(8,128)(2,1)}), bf16[32,64,128]{2,0,1:T(8,128)(2,1)S(1)}, u32[]{:S(2)}, u32[]{:S(2)}) async-start(bf16[32,64,128]{2,0,1:T(8,128)(2,1)} %copy.40), calls=%async_computation.2 | async-start | bytes 1048576 | tf_op jit(solution)/shard_map/all_to_all | solution.py:46
  40.2 23.1 %copy-start.5 = (bf16[32,64,128]{2,0,1:T(8,128)(2,1)}, bf16[32,64,128]{2,0,1:T(8,128)(2,1)S(1)}, u32[]{:S(2)}) copy-start(bf16[32,64,128]{2,0,1:T(8,128)(2,1)S(1)} %all-to-all-done.2) | copy-start | bytes 1572868
  40.2 21.1 %all-to-all-start.1 = ((bf16[32,64,128]{2,0,1:T(8,128)(2,1)}), bf16[32,64,128]{2,0,1:T(8,128)(2,1)S(1)}, u32[]{:S(2)}, u32[]{:S(2)}) async-start(bf16[32,64,128]{2,0,1:T(8,128)(2,1)} %copy.39), calls=%async_computation.1 | async-start | bytes 1048576 | tf_op jit(solution)/shard_map/all_to_all | solution.py:45
  44.9 27.1 %copy-start.9 = (bf16[1,128,512]{2,1,0:T(8,128)(2,1)S(1)}, bf16[1,128,512]{2,1,0:T(8,128)(2,1)}, u32[]{:S(2)}) copy-start(bf16[1,128,512]{2,1,0:T(8,128)(2,1)} %param.10) | copy-start | bytes 393220
  61.3 43.5 %copy-start.6 = (bf16[32,64,128]{2,0,1:T(8,128)(2,1)}, bf16[32,64,128]{2,0,1:T(8,128)(2,1)S(1)}, u32[]{:S(2)}) copy-start(bf16[32,64,128]{2,0,1:T(8,128)(2,1)S(1)} %all-to-all-done.1) | copy-start | bytes 1572868
  63.3 41.4 %all-to-all-start.3 = ((bf16[128,64,128]{2,0,1:T(8,128)(2,1)}), bf16[128,64,128]{2,0,1:T(8,128)(2,1)}, u32[]{:S(2)}, u32[]{:S(2)}) async-start(bf16[128,64,128]{2,0,1:T(8,128)(2,1)} %bitcast.12), calls=%async_computation.3 | async-start | bytes 4194304 | tf_op jit(solution)/shard_map/all_to_all | solution.py:48
  106.7 58.5 %all-to-all-start = ((bf16[128,64,128]{2,0,1:T(8,128)(2,1)}), bf16[128,64,128]{2,0,1:T(8,128)(2,1)S(1)}, u32[]{:S(2)}, u32[]{:S(2)}) async-start(bf16[128,64,128]{2,0,1:T(8,128)(2,1)} %bitcast.133), calls=%async_computation | async-start | bytes 4194304 | tf_op jit(solution)/shard_map/all_to_all | solution.py:47
  165.2 5.4 copy-start.10
  165.2 5.4 copy-start.11
  170.6 7.0 copy-start.3
  220.9 3.1 copy-start.2
  224.0 4.1 copy-start.1
  228.1 3.7 copy-start.4
  231.8 7.0 copy-start.3
  282.1 3.1 copy-start.2
  285.2 4.1 copy-start.1
  289.3 3.7 copy-start.4
  293.0 7.0 copy-start.3
  343.3 3.1 copy-start.2
  346.3 4.1 copy-start.1
  350.4 3.7 copy-start.4
  354.1 7.0 copy-start.3
  404.4 3.1 copy-start.2
  407.5 4.1 copy-start.1
  411.5 3.7 copy-start.4
  420.5 53.4 %all-to-all-start.5 = ((bf16[64,128,1,128]{1,3,2,0:T(8,128)(2,1)}), bf16[64,128,1,128]{1,3,2,0:T(8,128)(2,1)}, u32[]{:S(2)}, u32[]{:S(2)}) async-start(bf16[64,128,1,128]{1,3,2,0:T(8,128)(2,1)} %copy.46), calls=%async_computation.5 | async-start | bytes 4194304 | tf_op jit(solution)/shard_map/all_to_all | solution.py:114
  474.0 58.6 %all-to-all-start.6 = ((bf16[64,128,1,128]{1,3,2,0:T(8,128)(2,1)}), bf16[64,128,1,128]{1,3,2,0:T(8,128)(2,1)S(1)}, u32[]{:S(2)}, u32[]{:S(2)}) async-start(bf16[64,128,1,128]{1,3,2,0:T(8,128)(2,1)} %copy.50), calls=%async_computation.6 | async-start | bytes 4194304 | tf_op jit(solution)/shard_map/all_to_all | solution.py:121
  499.7 1373.3 %reduce-scatter.4.cloned.1.call-start = ((), (), s32[]{:S(2)}) async-start(), calls=%async_computation.8 | async-start | bytes 16842752
  558.4 1.0 copy-start.7
Sparse Core Ops, SparseCore 0:
  558.5 1314.3 reduce-scatter.3
where the time goes:
time: 1880 us
  waiting for transfers between devices  1430 us (76%)
  local copies, waits for them, and re-layouts  120 us (6%)
  matrix products  109 us (6%)
  starting transfers between devices  98.4 us (5%)
  other arithmetic  66.8 us (4%)
  blocking collectives  36.8 us (2%)
    unnamed x2, waiting for transfers between devices  1270 us
    convert_element_type x4, other arithmetic, one_block(): (probability * (dprob - row_delta) * score_scale).astype(jnp.bfloat16)  40.1 us
    dot_general x4, matrix products, one_block(): jnp.einsum('qhd,khd->hqk', grad_block, value_block, preferred_element_typ...  37.7 us
  transfers between devices with their start and end apart: 7, of which 7 were waited for; matrix products, arithmetic and copies ran while one was open for 1% of the time, Pallas kernels for 0%

commit v1 on v0

--- a/solution.py
+++ b/solution.py
@@ -45,7 +45,12 @@
         lax.all_to_all(query_units, "seq", split_axis=1, concat_axis=0, tiled=True),
         lax.all_to_all(grad_units, "seq", split_axis=1, concat_axis=0, tiled=True),
         lax.all_to_all(key_units, "seq", split_axis=1, concat_axis=0, tiled=True),
-        lax.all_to_all(value_units, "seq", split_axis=1, concat_axis=0, tiled=True),
+        jnp.concatenate(
+            lax.all_to_all(
+                jnp.stack(jnp.split(value_units, lax.axis_size("seq"), axis=1)), "seq", 0, 0
+            ),
+            axis=0,
+        ),
     )
     block_rows = min(512, seq_len // classes)
     blocks_seq = seq_len // classes // block_rows

time: 1880 us -> 1890 us (level)
  local copies, waits for them, and re-layouts: 120 us -> 159 us
  starting transfers between devices: 98.4 us -> 61.9 us
    unnamed x19 -> x80, local copies, waits for them, and re-layouts: 20 us -> 58.1 us
    unnamed x2, waiting for transfers between devices: 1270 us -> 1300 us
    all_to_all x1, starting transfers between devices: 25.7 us -> 5.08 us  [local(): lax.all_to_all(value_acc.reshape(seq_count, tokens_dev, 1, width_dev).ast...]
  transfers between devices with their start and end apart: 7 -> 7, of which waited for: 7 -> 6; matrix products, arithmetic and copies ran while one was open for 1% -> 3% of each run, Pallas kernels for 0% -> 0%
where the time goes in v1:
time: 1890 us; the launch traced here: 1880 us
  waiting for transfers between devices  1440 us (76%)
  local copies, waits for them, and re-layouts  159 us (8%)
  matrix products  107 us (6%)
  other arithmetic  66.8 us (4%)
  starting transfers between devices  61.9 us (3%)
  blocking collectives  25.7 us (1%)
    unnamed x2, waiting for transfers between devices  1300 us
    unnamed x80, local copies, waits for them, and re-layouts  58.1 us
    convert_element_type x4, other arithmetic, one_block(): (probability * (dprob - row_delta) * score_scale).astype(jnp.bfloat16)  40.1 us
    all_to_all x1, waiting for transfers between devices, local(): lax.all_to_all(value_acc.reshape(seq_count, tokens_dev, 1, width_dev).ast...  38.3 us
  transfers between devices with their start and end apart: 7, of which 6 were waited for; matrix products, arithmetic and copies ran while one was open for 3% of the time, Pallas kernels for 0%

profile of v1, /device:TPU:0, one launch (start us, length us, event | category | flops | bytes accessed | tf_op | source)
XLA Modules:
  0.0 1884.7 jit_solution(11210329596813361479)
XLA Ops:
  9.7 13.1 all-to-all-start.2
  63.5 12.9 all-to-all-start.1
  79.5 14.5 all-to-all-done.1
  93.9 4.7 all-to-all-start.3
  98.7 32.8 %all-to-all-done.3 = bf16[64,128,1,128]{3,1,2,0:T(8,128)(2,1)S(1)} async-done(((bf16[64,128,1,128]{3,1,2,0:T(8,128)(2,1)}), bf16[64,128,1,128]{3,1,2,0:T(8,128)(2,1)S(1)}, u32[]{:S(2)}, u32[]{:S(2)}) %all-to-all-start.3) | async-done | bytes 2097184 | tf_op jit(solution)/shard_map/all_to_all | solution.py:49
  133.5 20.5 %all-to-all-start = ((bf16[128,64,128]{2,0,1:T(8,128)(2,1)}), bf16[128,64,128]{2,0,1:T(8,128)(2,1)S(1)}, u32[]{:S(2)}, u32[]{:S(2)}) async-start(bf16[128,64,128]{2,0,1:T(8,128)(2,1)} %bitcast.385), calls=%async_computation | async-start | bytes 4194304 | tf_op jit(solution)/shard_map/all_to_all | solution.py:47
  154.0 32.8 %all-to-all-done = bf16[128,64,128]{2,0,1:T(8,128)(2,1)S(1)} async-done(((bf16[128,64,128]{2,0,1:T(8,128)(2,1)}), bf16[128,64,128]{2,0,1:T(8,128)(2,1)S(1)}, u32[]{:S(2)}, u32[]{:S(2)}) %all-to-all-start) | async-done | bytes 2097184 | tf_op jit(solution)/shard_map/all_to_all | solution.py:47
  192.1 242.2 %while.21 = (s32[]{:T(128)}, bf16[2048,1,128]{2,0,1:T(8,128)(2,1)}, f32[8192,1,128]{2,0,1:T(8,128)}, f32[8192,1,128]{2,0,1:T(8,128)}, bf16[8192,1,128]{2,0,1:T(8...) while((s32[]{:T(128)}, bf16[2048,1,128]{2,0,1:T(8,128)(2,1)}, ...), condition=%wide.region_4.5_spmd.clone.clone, body=%wide.region_0.4_spmd.clone.clone.sunk | while | flops 2746294784 | bytes 176347760 | solution.py:109
  195.4 3.8 fusion.57
  199.2 4.2 fusion.58
  203.4 8.8 multiply_reduce_fusion.2
  212.2 10.0 multiply_convert_fusion.2
  225.8 3.7 fusion.61
  231.4 3.1 constant_dynamic-slice_fusion.4
  236.3 5.5 fusion.60
  245.0 4.1 constant_dynamic-update-slice_fusion.70
  255.9 3.8 fusion.57
  259.7 4.2 fusion.58
  264.0 8.8 multiply_reduce_fusion.2
  272.8 10.0 multiply_convert_fusion.2
  286.4 3.7 fusion.61
  291.9 3.1 constant_dynamic-slice_fusion.4
  296.9 5.5 fusion.60
  305.5 4.1 constant_dynamic-update-slice_fusion.70
  316.5 3.8 fusion.57
  320.3 4.2 fusion.58
  324.6 8.8 multiply_reduce_fusion.2
  333.4 10.0 multiply_convert_fusion.2
  347.0 3.7 fusion.61
  352.5 3.1 constant_dynamic-slice_fusion.4
  357.5 5.5 fusion.60
  366.1 4.0 constant_dynamic-update-slice_fusion.70
  377.0 3.8 fusion.57
  380.8 4.2 fusion.58
  385.1 8.8 multiply_reduce_fusion.2
  393.9 10.0 multiply_convert_fusion.2
  407.5 3.7 fusion.61
  413.0 3.1 constant_dynamic-slice_fusion.4
  418.0 5.5 fusion.60
  426.6 4.0 constant_dynamic-update-slice_fusion.70
  439.6 5.6 all-to-all-start.5
  450.5 27.2 %all-to-all-done.5 = bf16[64,128,1,128]{1,3,2,0:T(8,128)(2,1)} async-done(((bf16[64,128,1,128]{1,3,2,0:T(8,128)(2,1)}), bf16[64,128,1,128]{1,3,2,0:T(8,128)(2,1)}, u32[]{:S(2)}, u32[]{:S(2)}) %all-to-all-start.5) | async-done | bytes 2097184 | tf_op jit(solution)/shard_map/all_to_all | solution.py:119
  477.7 5.1 all-to-all-start.6
  484.7 38.3 %all-to-all-done.6 = bf16[64,128,1,128]{1,3,2,0:T(8,128)(2,1)S(1)} async-done(((bf16[64,128,1,128]{1,3,2,0:T(8,128)(2,1)}), bf16[64,128,1,128]{1,3,2,0:T(8,128)(2,1)S(1)}, u32[]{:S(2)}, u32[]{:S(2)}) %all-to-all-start.6) | async-done | bytes 2097184 | tf_op jit(solution)/shard_map/all_to_all | solution.py:126
  523.4 8.1 convolution_bitcast_fusion.2
  531.5 17.4 copy.247
  550.0 25.7 %all_to_all.92 = bf16[64,32,1,128]{3,1,2,0:T(8,128)(2,1)S(1)} all-to-all(bf16[64,32,1,128]{3,1,2,0:T(8,128)(2,1)S(1)} %bitcast.454), channel_id=1, replica_groups=mesh['seq'=64,'dp'=4] {'seq'}, dimensions={0} | all-to-all | bytes 1048576 | tf_op jit(solution)/shard_map/all_to_all | solution.py:110
  578.4 1299.4 %reduce-scatter.4.cloned.1.call-done = f32[16,1024]{1,0:T(8,128)} async-done(((f32[4096,1024]{1,0:T(8,128)}), f32[16,1024]{1,0:T(8,128)}) %reduce-scatter.4.cloned.1.call-update) | async-done | bytes 65552
  (198 shorter events, 134.4 us)
Async XLA Ops:
  7.2 516.3 %copy-start = (bf16[1,128,4096]{2,1,0:T(8,128)(2,1)S(1)}, bf16[1,128,4096]{2,1,0:T(8,128)(2,1)}, u32[]{:S(2)}) copy-start(bf16[1,128,4096]{2,1,0:T(8,128)(2,1)} %param.13) | copy-start | bytes 3145732
  7.2 15.6 copy-start.8
  9.7 53.8 %all-to-all-start.2 = ((bf16[32,64,128]{2,0,1:T(8,128)(2,1)}), bf16[32,64,128]{2,0,1:T(8,128)(2,1)}, u32[]{:S(2)}, u32[]{:S(2)}) async-start(bf16[32,64,128]{2,0,1:T(8,128)(2,1)} %copy.229), calls=%async_computation.2 | async-start | bytes 1048576 | tf_op jit(solution)/shard_map/all_to_all | solution.py:46
  63.5 30.5 %all-to-all-start.1 = ((bf16[32,64,128]{2,0,1:T(8,128)(2,1)}), bf16[32,64,128]{2,0,1:T(8,128)(2,1)}, u32[]{:S(2)}, u32[]{:S(2)}) async-start(bf16[32,64,128]{2,0,1:T(8,128)(2,1)} %copy.228), calls=%async_computation.1 | async-start | bytes 1048576 | tf_op jit(solution)/shard_map/all_to_all | solution.py:45
  79.5 19.2 %copy-start.9 = (bf16[1,128,512]{2,1,0:T(8,128)(2,1)S(1)}, bf16[1,128,512]{2,1,0:T(8,128)(2,1)}, u32[]{:S(2)}) copy-start(bf16[1,128,512]{2,1,0:T(8,128)(2,1)} %param.10) | copy-start | bytes 393220
  93.9 37.5 %all-to-all-start.3 = ((bf16[64,128,1,128]{3,1,2,0:T(8,128)(2,1)}), bf16[64,128,1,128]{3,1,2,0:T(8,128)(2,1)S(1)}, u32[]{:S(2)}, u32[]{:S(2)}) async-start(bf16[64,128,1,128]{3,1,2,0:T(8,128)(2,1)} %constant_dynamic-update-slice_fusion.3), calls=%async_computation.3 | async-start | bytes 4194304 | tf_op jit(solution)/shard_map/all_to_all | solution.py:49
  131.5 2.0 copy-start.5
  133.5 53.3 %all-to-all-start = ((bf16[128,64,128]{2,0,1:T(8,128)(2,1)}), bf16[128,64,128]{2,0,1:T(8,128)(2,1)S(1)}, u32[]{:S(2)}, u32[]{:S(2)}) async-start(bf16[128,64,128]{2,0,1:T(8,128)(2,1)} %bitcast.385), calls=%async_computation | async-start | bytes 4194304 | tf_op jit(solution)/shard_map/all_to_all | solution.py:47
  189.0 3.1 copy-start.10
  189.0 3.1 copy-start.11
  192.2 7.0 copy-start.3
  199.2 4.3 copy-start.6
  241.9 3.1 copy-start.2
  244.9 4.1 copy-start.1
  249.0 3.7 copy-start.4
  252.7 7.0 copy-start.3
  259.7 4.3 copy-start.6
  302.5 3.1 copy-start.2
  305.5 4.1 copy-start.1
  309.6 3.7 copy-start.4
  313.3 7.0 copy-start.3
  320.3 4.3 copy-start.6
  363.0 3.1 copy-start.2
  366.1 4.0 copy-start.1
  370.1 3.7 copy-start.4
  373.8 7.0 copy-start.3
  380.8 4.3 copy-start.6
  423.5 3.1 copy-start.2
  426.6 4.0 copy-start.1
  430.7 3.7 copy-start.4
  439.6 38.0 %all-to-all-start.5 = ((bf16[64,128,1,128]{1,3,2,0:T(8,128)(2,1)}), bf16[64,128,1,128]{1,3,2,0:T(8,128)(2,1)}, u32[]{:S(2)}, u32[]{:S(2)}) async-start(bf16[64,128,1,128]{1,3,2,0:T(8,128)(2,1)} %copy.235), calls=%async_computation.5 | async-start | bytes 4194304 | tf_op jit(solution)/shard_map/all_to_all | solution.py:119
  477.7 45.4 %all-to-all-start.6 = ((bf16[64,128,1,128]{1,3,2,0:T(8,128)(2,1)}), bf16[64,128,1,128]{1,3,2,0:T(8,128)(2,1)S(1)}, u32[]{:S(2)}, u32[]{:S(2)}) async-start(bf16[64,128,1,128]{1,3,2,0:T(8,128)(2,1)} %copy.239), calls=%async_computation.6 | async-start | bytes 4194304 | tf_op jit(solution)/shard_map/all_to_all | solution.py:126
  482.7 1395.1 %reduce-scatter.4.cloned.1.call-start = ((), (), s32[]{:S(2)}) async-start(), calls=%async_computation.8 | async-start | bytes 16842752
  548.9 1.0 copy-start.7
Sparse Core Ops, SparseCore 0:
  549.1 1328.7 reduce-scatter.3
